TPU v7x, 512 devices: a whole 4x8x8 slice. The times are simulated.
512 devices in a mesh: row: 64 (over y_hi, x, z), col: 8 (over y_lo, core).
Axes of the slice: x: 4, y: 8 (y_hi: 2, y_lo: 4; y = y_hi * 4 + y_lo), z: 8, core: 2. Of those that a mesh axis runs over, the one named last changes fastest.
Arguments:
- features: bfloat16 [65536, 1024], P(('row', 'col')), may hold values from -6 to 6
- history: bfloat16 [65536, 1024], P(('row', 'col')), may hold values from -6 to 6
- degree: int32 [65536], P(('row', 'col')), may hold values from 8 to 64
- adj_tiles: bfloat16 [3072, 128, 128], P(('row', 'col')), may hold values from 0 to 3, as said below
- tile_index: int32 [3072], P(('row', 'col')), may hold values from 0 to 23, as said below
- tile_count: int32 [512], P(('row', 'col')), may hold values from 3 to 6, as said below
- weight: bfloat16 [1024, 1024], P(None, 'col'), may hold values from -0.1875 to 0.1875
- cotangent: bfloat16 [65536, 1024], P(('row', 'col')), may hold values from -6 to 6
Outputs:
- layer_out: bfloat16 [65536, 1024], P(('row', 'col'))
- grad_features: bfloat16 [65536, 1024], P(('row', 'col'))
- grad_weight: float32 [1024, 1024], P(None, 'col')
Inputs may be any that keep to these rules, and one draw needn't show every extreme that they name: `adj_tiles`: whole numbers: the edge counts of a tile's entries. Slots from tile_count on of a device are never read. `tile_index`: the codes of one device's 6 slots are distinct. Its first three slots hold tiles whose column block lies in the first, the last and the middle third of the 3 m column blocks, in that order. `tile_count`: some device has 6 live slots in every draw.
All inputs are finite; a program needn't handle non-finite values.
Results may differ from a plain program's by a relative error of at most 0.014.
Values may be sent and summed in bfloat16 or wider, within the bound.
No kernel may reach another device: no remote copies, remote signals or barrier semaphores. Data moves between devices by JAX's collectives and lax.ppermute only.
A program may use at most 64 MiB of HBM per device.

v0:
```python
import math
import jax
import jax.numpy as jnp
from jax import lax
from jax.sharding import PartitionSpec as P

TILE = 128


def padded_2(x, sides, width):
    for axis, dim in sides:
        count, length = (lax.axis_size(axis), x.shape[dim])
        up = [(i, (i + 1) % count) for i in range(count - 1)]
        down = [(j, i) for i, j in up]
        last = lax.slice_in_dim(x, length - width, length, axis=dim)
        initial = lax.slice_in_dim(x, 0, width, axis=dim)
        before = lax.ppermute(last, axis, up)
        after = lax.ppermute(initial, axis, down)
        x = jnp.concatenate([before, x, after], axis=dim)
    return x


def inverse_root(degree):
    return 1.0 / jnp.sqrt(degree.astype(jnp.float32))


def silu_slope(pre_act):
    sigmoid = jax.nn.sigmoid(pre_act)
    return sigmoid * (1.0 + pre_act * (1.0 - sigmoid))


def per_device(features, history, degree, adj_tiles, tile_index, tile_count, weight, cotangent):
    slab_rows = features.shape[0]
    col_count = lax.axis_size("col")
    blocks = slab_rows // TILE
    src_width = 3 * blocks
    part_rows = slab_rows * col_count
    own_scale = inverse_root(degree)
    own_src = (features.astype(jnp.float32) * own_scale[:, None]).astype(jnp.bfloat16)
    hist_src = (history.astype(jnp.float32) * own_scale[:, None]).astype(jnp.bfloat16)
    padded = padded_2(hist_src, (("row", 0),), slab_rows)
    sources = jnp.concatenate([padded[:slab_rows], own_src, padded[2 * slab_rows :]], axis=0)
    live_tiles = tile_count[0]

    def add_tile(slot_at, summed):
        tile_code = tile_index[slot_at]
        dest_block = tile_code // src_width
        src_block = tile_code % src_width
        source_rows = lax.dynamic_slice_in_dim(sources, src_block * TILE, TILE, 0)
        product = jnp.dot(adj_tiles[slot_at], source_rows, preferred_element_type=jnp.float32)
        current = lax.dynamic_slice_in_dim(summed, dest_block * TILE, TILE, 0)
        return lax.dynamic_update_slice_in_dim(summed, current + product, dest_block * TILE, 0)

    partial_sum = lax.fori_loop(
        0, live_tiles, add_tile, jnp.zeros((part_rows, features.shape[1]), jnp.float32)
    )
    aggregate_raw = lax.psum_scatter(
        partial_sum.astype(jnp.bfloat16), "col", scatter_dimension=0, tiled=True
    ).astype(jnp.float32)
    aggregated = (aggregate_raw * own_scale[:, None]).astype(jnp.bfloat16)
    whole_weight = lax.all_gather(weight, "col", axis=1, tiled=True)
    pre_act = jnp.dot(aggregated, whole_weight, preferred_element_type=jnp.float32)
    layer_out = jax.nn.silu(pre_act).astype(jnp.bfloat16)
    grad_pre = (cotangent.astype(jnp.float32) * silu_slope(pre_act)).astype(jnp.bfloat16)
    back_prop = lax.dot_general(
        grad_pre, whole_weight, (((1,), (1,)), ((), ())), preferred_element_type=jnp.float32
    )
    dest_grad = (back_prop * own_scale[:, None]).astype(jnp.bfloat16)
    all_dest = lax.all_gather(dest_grad, "col", axis=0, tiled=True)

    def add_grad(slot_at, summed):
        tile_code = tile_index[slot_at]
        dest_block = tile_code // src_width
        src_block = tile_code % src_width - blocks
        inside = (src_block >= 0) & (src_block < blocks)

        def accumulate(running):
            dest_rows = lax.dynamic_slice_in_dim(all_dest, dest_block * TILE, TILE, 0)
            product = lax.dot_general(
                adj_tiles[slot_at],
                dest_rows,
                (((0,), (0,)), ((), ())),
                preferred_element_type=jnp.float32,
            )
            return running + product

        def unchanged(running):
            return running

        return lax.cond(inside, accumulate, unchanged, summed)

    grad_sum = lax.fori_loop(0, live_tiles, add_grad, jnp.zeros(features.shape, jnp.float32))
    grad_features = (grad_sum * own_scale[:, None]).astype(jnp.bfloat16)
    node_total = part_rows * lax.axis_size("row")
    loss_scale = 1.0 / math.sqrt(node_total)
    out_cols = weight.shape[1]
    local_term = lax.dot_general(
        aggregated, grad_pre, (((0,), (0,)), ((), ())), preferred_element_type=jnp.float32
    )
    summed_all = lax.psum(local_term, ("row", "col"))
    grad_weight = (
        lax.dynamic_slice_in_dim(summed_all, lax.axis_index("col") * out_cols, out_cols, 1)
        * loss_scale
    )
    return (layer_out, grad_features, grad_weight)


def solution(mesh):
    in_specs = (
        P(("row", "col"), None),
        P(("row", "col"), None),
        P(("row", "col")),
        P(("row", "col"), None, None),
        P(("row", "col")),
        P(("row", "col")),
        P(None, "col"),
        P(("row", "col"), None),
    )
    out_specs = (P(("row", "col"), None), P(("row", "col"), None), P(None, "col"))
    return jax.shard_map(
        per_device, mesh=mesh, in_specs=in_specs, out_specs=out_specs, check_vma=False
    )
```

profile of v0, /device:TPU:135, one launch (start us, length us, event | category | flops | bytes accessed | tf_op | source)
XLA Modules:
  0.0 481.6 jit_solution(10469675945475615984)
XLA Ops:
  7.2 0.7 all-gather.3.cloned.1.call-update
  7.9 0.7 convert_rsqrt_fusion
  8.6 1.2 multiply_convert_fusion.4
  9.8 4.0 collective-permute-start
  13.8 1.9 collective-permute-start.1
  15.7 3.1 collective-permute-done
  18.9 5.9 %collective-permute-done.1 = bf16[128,1024]{1,0:T(8,128)(2,1)S(1)} collective-permute-done((bf16[128,1024]{1,0:T(8,128)(2,1)S(1)}, bf16[128,1024]{1,0:T(8,128)(2,1)S(1)}, u32[]{:S(2)}, u32[]{:S(2)}) %collective-permute-start.1) | collective-permute-done | bytes 262176 | tf_op jit(solution)/shard_map/ppermute | solution.py:18
  24.7 0.1 pad_maximum_fusion
  24.8 2.5 broadcast_in_dim.4
  27.3 32.6 %while.28 = (s32[]{:T(128)}, f32[1024,1024]{1,0:T(8,128)}, s32[]{:T(128)}, s32[6]{0:T(128)S(1)}, bf16[6,128,128]{2,1,0:T(8,128)(2,1)}, /*index=5*/bf16[384,1024]...) while((s32[]{:T(128)}, f32[1024,1024]{1,0:T(8,128)}, ...), condition=%wide.region_1.2_spmd, body=%wide.region_0.1_spmd.sunk | while | flops 33685528 | bytes 1343902 | solution.py:54
  28.0 0.6 dynamic_slice.63
  30.5 2.1 fusion.19
  33.3 0.6 dynamic_slice.63
  35.8 2.1 fusion.19
  38.6 0.6 dynamic_slice.63
  41.2 2.1 fusion.19
  43.9 0.6 dynamic_slice.63
  46.5 2.1 fusion.19
  49.3 0.6 dynamic_slice.63
  51.8 2.1 fusion.19
  54.6 0.6 dynamic_slice.63
  57.2 2.1 fusion.19
  59.9 3.9 convert_element_type.51
  63.8 0.0 all-reduce.2.cloned.1.call-start
  63.9 51.4 %reduce-scatter.2.cloned.1.call-done = bf16[128,1024]{1,0:T(8,128)(2,1)} async-done(((bf16[1024,1024]{1,0:T(8,128)(2,1)}), bf16[128,1024]{1,0:T(8,128)(2,1)}) %reduce-scatter.2.cloned.1.call-update) | async-done | bytes 262160 | tf_op jit(solution)/shard_map/reduce_scatter | solution.py:57
  115.3 3.0 multiply_convert_fusion.2
  118.3 2.8 fusion.10
  121.2 1.5 copy-done.2
  122.8 1.6 fusion.9
  124.3 285.7 %all-reduce.2.cloned.1.call-done = f32[1024,1024]{1,0:T(8,128)} async-done(((f32[1024,1024]{1,0:T(8,128)}), f32[1024,1024]{1,0:T(8,128)}) %all-reduce.2.cloned.1.call-update) | async-done | bytes 4194320 | tf_op jit(solution)/shard_map/psum | solution.py:100
  410.0 1.9 dynamic-slice_multiply_fusion
  411.9 37.2 %all-gather.5.cloned.1.call-done = bf16[1024,1024]{1,0:T(8,128)(2,1)} async-done(((bf16[128,1024]{1,0:T(8,128)(2,1)}), bf16[1024,1024]{1,0:T(8,128)(2,1)}) %all-gather.5.cloned.1.call-update) | async-done | bytes 2097168 | tf_op jit(solution)/shard_map/all_gather | solution.py:69
  449.1 25.2 %while.29 = (s32[]{:T(128)}, f32[128,1024]{1,0:T(8,128)S(1)}, s32[]{:T(128)}, s32[6]{0:T(128)S(1)}, bf16[6,128,128]{2,1,0:T(8,128)(2,1)}, /*index=5*/bf16[1024,1...) while((s32[]{:T(128)}, f32[128,1024]{1,0:T(8,128)S(1)}, s32[]{:T(128)}, ...), condition=%wide.region_6.7_spmd, body=%wide.region_3.6_spmd.sunk | while | flops 33685536 | bytes 1343953 | solution.py:92
  449.8 0.6 dynamic_slice.64
  451.7 0.6 dynamic_slice.64
  453.7 0.6 dynamic_slice.64
  454.9 3.2 conditional.2
  456.9 1.2 convolution_add_fusion.1
  458.8 0.6 dynamic_slice.64
  460.1 3.2 conditional.2
  462.1 1.2 convolution_add_fusion.1
  464.0 0.6 dynamic_slice.64
  465.2 3.2 conditional.2
  467.2 1.2 convolution_add_fusion.1
  469.1 0.6 dynamic_slice.64
  470.4 3.2 conditional.2
  472.4 1.2 convolution_add_fusion.1
  474.3 0.8 multiply_convert_fusion
  (17 shorter events, 0.3 us)
Async XLA Ops:
  7.2 56.7 %all-gather.3.cloned.1.call-start = ((), (), s32[]{:S(2)}) async-start(), calls=%async_computation.2 | async-start | bytes 2359296 | tf_op jit(solution)/shard_map/all_gather | solution.py:61
  7.9 107.4 %reduce-scatter.2.cloned.1.call-start = ((), (), s32[]{:S(2)}) async-start(), calls=%async_computation.1 | async-start | bytes 2359296 | tf_op jit(solution)/shard_map/reduce_scatter | solution.py:57
  9.8 9.1 %collective-permute-start = (bf16[128,1024]{1,0:T(8,128)(2,1)S(1)}, bf16[128,1024]{1,0:T(8,128)(2,1)S(1)}, u32[]{:S(2)}, u32[]{:S(2)}) collective-permute-start(bf16[128,1024]{1,0:T(8,128)(2,1)S(1)} %get-tuple-element.260), channel_id=1, source_target_pairs={{0,8},{8,16},{16,24},{24,32},{32,40},{40,48},{48,56},{56,64},{64,7... | collective-permute-start | bytes 786440 | tf_op jit(solution)/shard_map/ppermute | solution.py:17
  13.8 10.9 %collective-permute-start.1 = (bf16[128,1024]{1,0:T(8,128)(2,1)S(1)}, bf16[128,1024]{1,0:T(8,128)(2,1)S(1)}, u32[]{:S(2)}, u32[]{:S(2)}) collective-permute-start(bf16[128,1024]{1,0:T(8,128)(2,1)S(1)} %get-tuple-element.260), channel_id=1, source_target_pairs={{8,0},{16,8},{24,16},{32,24},{40,32},{48,40},{56,48},{64,56},{72,6... | collective-permute-start | bytes 786440 | tf_op jit(solution)/shard_map/ppermute | solution.py:18
  24.8 2.5 copy-start.3
  63.8 54.5 %copy-start = (bf16[128,1024]{1,0:T(8,128)(2,1)S(1)}, bf16[128,1024]{1,0:T(8,128)(2,1)}, u32[]{:S(2)}) copy-start(bf16[128,1024]{1,0:T(8,128)(2,1)} %param.21) | copy-start | bytes 786436
  63.8 346.2 %all-reduce.2.cloned.1.call-start = ((), (), s32[]{:S(2)}) async-start(), calls=%async_computation.4 | async-start | bytes 8388608 | tf_op jit(solution)/shard_map/psum | solution.py:100
  115.3 3.0 copy-start.1
  121.2 1.6 copy-start.2
  121.2 327.9 %all-gather.5.cloned.1.call-start = ((), (), s32[]{:S(2)}) async-start(), calls=%async_computation.3 | async-start | bytes 2359296 | tf_op jit(solution)/shard_map/all_gather | solution.py:69
Sparse Core Ops, SparseCore 0:
  10.0 44.7 all-gather.2
  63.9 51.3 reduce-scatter.1
  121.3 288.6 all-reduce.1
  412.5 36.5 all-gather.4
where the time goes:
time: 483 us; the launch traced here: 482 us
  waiting for transfers between devices  384 us (80%)
  loops' own time  33.2 us (7%)
  matrix products  24.9 us (5%)
  between operations  13.8 us (3%)
  local copies, waits for them, and re-layouts  11.1 us (2%)
  other arithmetic  8.45 us (2%)
  starting transfers between devices  6.08 us (1%)
    psum x1, waiting for transfers between devices, per_device(): summed_all = lax.psum(local_term, ('row', 'col'))  286 us
    reduce_scatter x1, waiting for transfers between devices, per_device(): lax.psum_scatter(partial_sum.astype(jnp.bfloat16), 'col', scatter_dimensi...  51.4 us
    all_gather x1, waiting for transfers between devices, per_device(): all_dest = lax.all_gather(dest_grad, 'col', axis=0, tiled=True)  37.2 us
    another operation x1, loops' own time, per_device(): lax.fori_loop(0, live_tiles, add_tile, jnp.zeros((part_rows, features.sha...  16.5 us
    dot_general x6, matrix products, add_tile(): jnp.dot(adj_tiles[slot_at], source_rows, preferred_element_type=jnp.float32)  12.6 us
  transfers between devices with their start and end apart: 6, of which 5 were waited for; matrix products, arithmetic and copies ran while one was open for 6% of the time, Pallas kernels for 0%

commit v1 on v0

--- a/solution.py
+++ b/solution.py
@@ -97,7 +97,7 @@
     local_term = lax.dot_general(
         aggregated, grad_pre, (((0,), (0,)), ((), ())), preferred_element_type=jnp.float32
     )
-    summed_all = lax.psum(local_term, ("row", "col"))
+    summed_all = lax.psum(lax.psum(local_term, "col"), "row")
     grad_weight = (
         lax.dynamic_slice_in_dim(summed_all, lax.axis_index("col") * out_cols, out_cols, 1)
         * loss_scale

time: 483 us -> 1150 us (2.38)
  the two profiles are of different devices: /device:TPU:135 before, /device:TPU:8 now
where the time goes in v1:
time: 1150 us
  waiting for transfers between devices  1070 us (93%)
  loops' own time  25.3 us (2%)
  matrix products  20.3 us (2%)
  between operations  13.8 us (1%)
    psum x2, waiting for transfers between devices, per_device(): summed_all = lax.psum(lax.psum(local_term, 'col'), 'row')  958 us
    reduce_scatter x1, waiting for transfers between devices, per_device(): lax.psum_scatter(partial_sum.astype(jnp.bfloat16), 'col', scatter_dimensi...  56 us
    all_gather x1, waiting for transfers between devices, per_device(): all_dest = lax.all_gather(dest_grad, 'col', axis=0, tiled=True)  43 us
  transfers between devices with their start and end apart: 7, of which 7 were waited for; matrix products, arithmetic and copies ran while one was open for 3% of the time, Pallas kernels for 0%

profile of v1, /device:TPU:8, one launch (start us, length us, event | category | flops | bytes accessed | tf_op | source)
XLA Modules:
  0.0 1152.7 jit_solution(13738026002796385310)
XLA Ops:
  7.2 0.0 all-gather.3.cloned.1.call-start
  7.2 0.7 all-gather.3.cloned.1.call-update
  7.9 0.0 reduce-scatter.2.cloned.1.call-start
  7.9 0.7 convert_rsqrt_fusion
  8.6 1.2 multiply_convert_fusion.4
  9.8 4.3 collective-permute-start
  14.1 1.3 collective-permute-start.1
  15.4 4.2 collective-permute-done
  19.6 4.8 collective-permute-done.1
  24.4 0.1 pad_maximum_fusion
  24.4 2.5 broadcast_in_dim.4
  26.9 27.3 %while.28 = (s32[]{:T(128)}, f32[1024,1024]{1,0:T(8,128)}, s32[]{:T(128)}, s32[6]{0:T(128)S(1)}, bf16[6,128,128]{2,1,0:T(8,128)(2,1)}, /*index=5*/bf16[384,1024]...) while((s32[]{:T(128)}, f32[1024,1024]{1,0:T(8,128)}, ...), condition=%wide.region_1.2_spmd, body=%wide.region_0.1_spmd.sunk | while | flops 33685528 | bytes 1343902 | solution.py:54
  27.6 0.6 dynamic_slice.63
  30.2 2.1 fusion.19
  32.9 0.6 dynamic_slice.63
  35.5 2.1 fusion.19
  38.3 0.6 dynamic_slice.63
  40.8 2.1 fusion.19
  43.6 0.6 dynamic_slice.63
  46.2 2.1 fusion.19
  48.9 0.6 dynamic_slice.63
  51.5 2.1 fusion.19
  54.3 3.9 convert_element_type.51
  58.2 0.0 reduce-scatter.2.cloned.1.call-update
  58.2 0.0 all-reduce.3.cloned.1.call-start
  58.3 1.9 all-gather.3.cloned.1.call-done
  60.2 56.0 %reduce-scatter.2.cloned.1.call-done = bf16[128,1024]{1,0:T(8,128)(2,1)} async-done(((bf16[1024,1024]{1,0:T(8,128)(2,1)}), bf16[128,1024]{1,0:T(8,128)(2,1)}) %reduce-scatter.2.cloned.1.call-update) | async-done | bytes 262160 | tf_op jit(solution)/shard_map/reduce_scatter | solution.py:57
  116.1 3.0 multiply_convert_fusion.2
  119.1 2.9 fusion.10
  122.0 0.0 all-gather.5.cloned.1.call-start
  122.0 1.5 copy-done.2
  123.5 1.6 fusion.9
  125.1 0.0 all-reduce.5.cloned.1.call-start
  125.2 110.5 %all-reduce.3.cloned.1.call-done = f32[1024,1024]{1,0:T(8,128)} async-done(((f32[1024,1024]{1,0:T(8,128)}), f32[1024,1024]{1,0:T(8,128)}) %all-reduce.3.cloned.1.call-update) | async-done | bytes 4194320 | tf_op jit(solution)/shard_map/psum | solution.py:100
  235.7 43.0 %all-gather.5.cloned.1.call-done = bf16[1024,1024]{1,0:T(8,128)(2,1)} async-done(((bf16[128,1024]{1,0:T(8,128)(2,1)}), bf16[1024,1024]{1,0:T(8,128)(2,1)}) %all-gather.5.cloned.1.call-update) | async-done | bytes 2097168 | tf_op jit(solution)/shard_map/all_gather | solution.py:69
  278.8 16.8 %while.29 = (s32[]{:T(128)}, f32[128,1024]{1,0:T(8,128)S(1)}, s32[]{:T(128)}, s32[6]{0:T(128)S(1)}, bf16[6,128,128]{2,1,0:T(8,128)(2,1)}, /*index=5*/bf16[1024,1...) while((s32[]{:T(128)}, f32[128,1024]{1,0:T(8,128)S(1)}, s32[]{:T(128)}, ...), condition=%wide.region_6.7_spmd, body=%wide.region_3.6_spmd.sunk | while | flops 33685536 | bytes 1343953 | solution.py:92
  279.4 0.6 dynamic_slice.64
  281.4 0.6 dynamic_slice.64
  283.3 0.6 dynamic_slice.64
  284.6 3.2 conditional.2
  286.6 1.2 convolution_add_fusion.1
  288.5 0.6 dynamic_slice.64
  290.4 0.6 dynamic_slice.64
  291.7 3.2 conditional.2
  293.7 1.2 convolution_add_fusion.1
  295.5 0.8 multiply_convert_fusion
  296.3 847.9 %all-reduce.5.cloned.1.call-done = f32[1024,1024]{1,0:T(8,128)} async-done(((f32[1024,1024]{1,0:T(8,128)}), f32[1024,1024]{1,0:T(8,128)}) %all-reduce.5.cloned.1.call-update) | async-done | bytes 4194320 | tf_op jit(solution)/shard_map/psum | solution.py:100
  1144.3 1.9 dynamic-slice_multiply_fusion
  (14 shorter events, 0.1 us)
Async XLA Ops:
  7.2 53.0 %all-gather.3.cloned.1.call-start = ((), (), s32[]{:S(2)}) async-start(), calls=%async_computation.2 | async-start | bytes 2359296 | tf_op jit(solution)/shard_map/all_gather | solution.py:61
  7.9 108.2 %reduce-scatter.2.cloned.1.call-start = ((), (), s32[]{:S(2)}) async-start(), calls=%async_computation.1 | async-start | bytes 2359296 | tf_op jit(solution)/shard_map/reduce_scatter | solution.py:57
  9.8 9.8 collective-permute-start
  14.1 10.3 collective-permute-start.1
  24.4 2.5 copy-start.3
  58.2 60.9 %copy-start = (bf16[128,1024]{1,0:T(8,128)(2,1)S(1)}, bf16[128,1024]{1,0:T(8,128)(2,1)}, u32[]{:S(2)}) copy-start(bf16[128,1024]{1,0:T(8,128)(2,1)} %param.21) | copy-start | bytes 786436
  58.2 177.5 %all-reduce.3.cloned.1.call-start = ((), (), s32[]{:S(2)}) async-start(), calls=%async_computation.4 | async-start | bytes 8388608 | tf_op jit(solution)/shard_map/psum | solution.py:100
  116.1 3.0 copy-start.1
  122.0 1.6 copy-start.2
  122.0 156.7 %all-gather.5.cloned.1.call-start = ((), (), s32[]{:S(2)}) async-start(), calls=%async_computation.3 | async-start | bytes 2359296 | tf_op jit(solution)/shard_map/all_gather | solution.py:69
  125.1 1019.1 %all-reduce.5.cloned.1.call-start = ((), (), s32[]{:S(2)}) async-start(), calls=%async_computation.5 | async-start | bytes 8388608 | tf_op jit(solution)/shard_map/psum | solution.py:100
Sparse Core Ops, SparseCore 0:
  10.0 50.1 all-gather.2
  63.0 53.0 reduce-scatter.1
  122.1 113.5 all-reduce.2
  238.2 40.4 all-gather.4
  281.5 862.7 all-reduce.4
